TPU v7x, 256 devices: a whole 4x4x8 slice. The times are simulated.
256 devices in a mesh: grp: 8 (over z), blk: 32 (over y, x, core).
Axes of the slice: x: 4, y: 4, z: 8, core: 2. Of those that a mesh axis runs over, the one named last changes fastest.
Arguments:
- embeddings: bfloat16 [8, 2048, 1024], P('grp', 'blk'), may hold values from -72 to 72
- cluster_ids: int32 [8, 2048], P('grp', 'blk'), may hold values from 0 to 63, never falling along the last dimension, each value on 1 to 128 neighbouring positions
- block_list: int32 [8, 256, 2], P('grp', 'blk'), may hold values from 0 to 31, as said below
- block_counts: int32 [8, 32], P('grp', 'blk'), may hold values from 1 to 8, as said below
- pair_targets: float32 [8, 256, 4096], P('grp', 'blk'), may hold values from -6 to 6
- w_left: bfloat16 [1024, 512], replicated, may hold values from -0.125 to 0.125
- w_right: bfloat16 [1024, 512], replicated, may hold values from -0.125 to 0.125
- hidden_bias: float32 [512], replicated, may hold values from -3 to 3
- w_middle: bfloat16 [512, 128], replicated, may hold values from -0.25 to 0.25
- w_final: float32 [128], replicated, may hold values from -0.5 to 0.5
Outputs:
- grad_embeddings: float32 [8, 2048, 1024], P('grp', 'blk')
- grad_left: float32 [1024, 512], replicated
- grad_right: float32 [1024, 512], replicated
- grad_bias: float32 [512], replicated
- grad_middle: float32 [512, 128], replicated
- grad_final: float32 [128], replicated
Inputs may be any that keep to these rules, and one draw needn't show every extreme that they name: `block_list`: entries are panels of the device's own group; the column panel lies within one of the row panel. `block_counts`: slots of a device at and beyond its count are unused; in every group one device has exactly 8.
All inputs are finite; a program needn't handle non-finite values.
Results may differ from a plain program's by a relative error of at most 0.012.
Values may be sent and summed in bfloat16 or wider, within the bound.
No kernel may reach another device: no remote copies, remote signals or barrier semaphores. Data moves between devices by JAX's collectives and lax.ppermute only.
A program may use at most 128 MiB of HBM per device.

v0:
```python
import math

import jax
import jax.numpy as jnp
from jax import lax
from jax.experimental import pallas as pl
from jax.experimental.pallas import tpu as pltpu
from jax.sharding import PartitionSpec as P

PANEL = 64
B_DEV = 8
ROWS = 8
CHUNK = 256
BF = jnp.bfloat16
F32 = jnp.float32


def forward(tile_at, left_s, right_s, hid_s, slope_s, rows=range(ROWS)):
    k = tile_at // 8
    left8 = left_s[pl.ds(pl.multiple_of(tile_at % 8 * ROWS, ROWS), ROWS), :]
    right = right_s[pl.ds(pl.multiple_of(k * PANEL, PANEL), PANEL), :]
    for a in rows:
        part = slice(a * PANEL, (a + 1) * PANEL)
        u = right.astype(BF) + jnp.broadcast_to(left8[a : a + 1, :], right.shape).astype(BF)
        p = jnp.tanh(u) + BF(1.0)
        h = u * p
        hid_s[part, :] = h
        slope_s[part, :] = p + h * (BF(2.0) - p)


def backward(
    tile_at, hid_s, slope_s, info_s, half_s, wmt_ref, wf_ref, lacc, racc, mid_acc, fin_acc
):
    col0 = pl.multiple_of(tile_at // 8 * PANEL, PANEL)
    row0 = pl.multiple_of(tile_at % 8 * ROWS, ROWS)
    wf = wf_ref[...]
    parts = [slice(c * CHUNK, (c + 1) * CHUNK) for c in range(ROWS * PANEL // CHUNK)]
    pre = [
        jnp.dot(hid_s[part, :], half_s[...], preferred_element_type=F32).T
        for part in parts
    ]
    terms, hiddens, fins = [], [], []
    for part, u in zip(parts, pre):
        p = jnp.tanh(u) + 1.0
        act = u * p
        predicted = jnp.sum(act * wf, axis=0, keepdims=True)
        pair_slope = info_s[tile_at, 1:2, part] * (
            info_s[tile_at, 2:3, part] * predicted - info_s[tile_at, 0:1, part]
        )
        grad_second = ((0.5 * pair_slope) * wf * (p + act * (2.0 - p))).astype(BF)
        fin = act * pair_slope
        fins.append(sum(fin[:, j * 128 : (j + 1) * 128] for j in range(CHUNK // 128)))
        hiddens.append(
            lax.dot_general(grad_second, wmt_ref[...], (((0,), (0,)), ((), ())), preferred_element_type=F32)
        )
        terms.append(jnp.dot(grad_second, hid_s[part, :], preferred_element_type=F32))
    fin_acc[...] += sum(fins)
    cols, rows = None, []
    for part, grad_hidden in zip(parts, hiddens):
        for a in range(CHUNK // PANEL):
            at = slice(part.start + a * PANEL, part.start + (a + 1) * PANEL)
            g = grad_hidden[a * PANEL : (a + 1) * PANEL, :] * slope_s[at, :].astype(F32)
            rows.append(jnp.sum(g, axis=0, keepdims=True))
            cols = g if cols is None else cols + g
    mid_acc[...] += sum(terms)
    racc[pl.ds(col0, PANEL), :] += cols
    lacc[pl.ds(row0, ROWS), :] += jnp.concatenate(rows, axis=0)


def pair_kernel(
    core,
    ids_s,
    ids_ref,
    left_ref,
    right_o,
    right_m,
    right_p,
    targets_ref,
    bias_ref,
    wmt_ref,
    wf_ref,
    out_left,
    out_outer,
    out_own,
    out_keep,
    out_sent,
    todo,
    panels_s,
    sems,
    left_s,
    right_s,
    info_s,
    half_s,
    hid_s,
    slope_s,
    lacc,
    racc,
    mid_acc,
    fin_acc,
):
    hidden = left_ref.shape[1]
    tile = ROWS * PANEL
    loads = [
        pltpu.make_async_copy(ref.at[0:PANEL, :], panels_s.at[n], sems.at[m])
        for m, (n, ref) in enumerate(
            ((0, left_ref), (1 + 2 * core[0], right_o), (2, right_m), (3 - 2 * core[0], right_p))
        )
    ]
    for copy in loads:
        copy.start()
    iota = lambda shape, axis: lax.broadcasted_iota(jnp.int32, shape, axis)
    begin = jnp.sum(jnp.where((ids_ref[...] < ids_s[1, PANEL // 2].astype(F32)) & (iota((8, PANEL), 0) < 3), 1, 0))
    shift = PANEL - (begin & (PANEL - 1))

    def scan(i, n):
        j, rt = i // 8, i % 8
        start = jnp.maximum(j * PANEL - shift, 0)
        end = jnp.minimum(j * PANEL - shift + PANEL - 1, 3 * PANEL - 1)
        last = jnp.maximum(end, 0)
        meets = (
            (end >= 0)
            & (ids_s[1, rt * ROWS] <= ids_s[last // PANEL, last % PANEL])
            & (ids_s[start // PANEL, start % PANEL] <= ids_s[1, rt * ROWS + ROWS - 1])
        )
        todo[n] = i
        return n + meets.astype(jnp.int32)

    n_todo = lax.fori_loop(0, 32, scan, 0)
    half_s[...] = (wmt_ref[...].astype(F32) * 0.5).T.astype(BF)
    n_src = targets_ref.shape[0]
    tsum = jnp.dot(
        (iota((24, n_src), 1) % 24 == iota((24, n_src), 0)).astype(BF), targets_ref[...], preferred_element_type=F32
    )
    ids = ids_ref[...]
    spread = (iota((PANEL, tile), 0) % ROWS == iota((PANEL, tile), 1) // PANEL).astype(BF)
    repeat = (iota((PANEL, tile), 0) == iota((PANEL, tile), 1) % PANEL).astype(BF)
    row_ids = jnp.where(iota((8, PANEL), 1) // ROWS == iota((8, PANEL), 0), ids[1:2, :], 0.0)
    row_ids = jnp.dot(row_ids.astype(BF), spread, preferred_element_type=F32)
    col_ids = jnp.dot(ids.astype(BF), repeat, preferred_element_type=F32)
    lane = iota((8, tile), 1)
    itself = iota((8, tile), 0) * ROWS + lane // PANEL == lane % PANEL
    infos = []
    for k in range(3):
        same = row_ids == col_ids[k : k + 1, :]
        mask = jnp.where(same & ~itself if k == 1 else same, 16.0, 0.0)
        count = jnp.max(
            jnp.where(iota((1, tile), 1) == k * (PANEL + 1), tsum[8:9, :], 0.0), axis=1, keepdims=True
        )
        infos.append((tsum[k * 8 : k * 8 + 8, :], mask, jnp.broadcast_to(count, (8, tile))))
    ahead, behind = lax.rem(shift, tile), lax.rem(shift + tile - PANEL, tile)
    for j in range(4):
        for n in range(3):
            here = pltpu.roll(infos[j][n], ahead, 1) if j < 3 else jnp.zeros((8, tile), F32)
            before = pltpu.roll(infos[j - 1][n], behind, 1) if j > 0 else jnp.zeros((8, tile), F32)
            moved = jnp.where(lane % PANEL >= shift, here, before)
            for rt in range(8):
                info_s[j * 8 + rt, n : n + 1, :] = moved[rt : rt + 1, :]
    lacc[...] = jnp.zeros_like(lacc)
    racc[...] = jnp.zeros_like(racc)
    mid_acc[...] = jnp.zeros_like(mid_acc)
    fin_acc[...] = jnp.zeros_like(fin_acc)
    for copy in loads:
        copy.wait()
    left_s[...] = (panels_s[0].astype(F32) + bias_ref[...]) * 0.5
    place = (iota((4 * PANEL, 3 * PANEL), 0) == iota((4 * PANEL, 3 * PANEL), 1) + shift).astype(BF)
    rights = jnp.concatenate([panels_s[k + 1] for k in range(3)], axis=0)
    right_s[...] = jnp.dot(place, rights, preferred_element_type=F32) * 0.5
    rest = (info_s, half_s, wmt_ref, wf_ref, lacc, racc, mid_acc, fin_acc)

    def step(i, carry):
        forward(todo[i], left_s, right_s, hid_s, slope_s)
        backward(todo[i], hid_s, slope_s, *rest)
        return carry

    lax.fori_loop(0, n_todo, step, 0)
    left = lacc[...] * 0.5
    out_left[...] = left.astype(BF)
    back = (iota((3 * PANEL, 4 * PANEL), 1) == iota((3 * PANEL, 4 * PANEL), 0) + shift).astype(BF)
    total = racc[...] * 0.5
    high = total.astype(BF)
    low = (total - high.astype(F32)).astype(BF)
    right_s[0 : 3 * PANEL, :] = jnp.dot(back, high, preferred_element_type=F32) + jnp.dot(
        back, low, preferred_element_type=F32
    )
    at = pl.multiple_of(2 * PANEL * core[0], PANEL)
    outer = right_s[pl.ds(at, PANEL), :].astype(BF)
    own = right_s[PANEL : 2 * PANEL, :].astype(BF)
    partner = right_s[pl.ds(pl.multiple_of(2 * PANEL - at, PANEL), PANEL), :].astype(BF)
    out_outer[...] = outer
    out_own[...] = own
    out_sent[PANEL : 2 * PANEL, :] = partner

    def middle(ref, start):
        for j in range(hidden // 128):
            block = slice(j * 128, (j + 1) * 128)
            ref[start : start + 128, block] = mid_acc[:, block].T.astype(BF)

    def small(ref, start):
        ref[start : start + 128, :] = jnp.zeros((128, hidden), BF)
        ref[start : start + 1, :] = jnp.sum(left, axis=0, keepdims=True).astype(BF)
        ref[start + 16 : start + 17, 0:128] = jnp.sum(fin_acc[...].T, axis=0, keepdims=True).astype(BF)

    @pl.when(core[0] == 0)
    def _():
        out_sent[0:PANEL, :] = own
        small(out_sent, 2 * PANEL)
        middle(out_keep, 0)

    @pl.when(core[0] != 0)
    def _():
        out_sent[0:PANEL, :] = left.astype(BF)
        middle(out_sent, 2 * PANEL)
        small(out_keep, 0)


def pair_grads(core, ids_s, ids, left, right_o, right_m, right_p, targets, bias, wmt, wf):
    hidden = left.shape[1]
    upper = wmt.shape[0]
    tile = ROWS * PANEL
    vmem = pl.BlockSpec(memory_space=pltpu.VMEM)
    panel = jax.ShapeDtypeStruct((PANEL, hidden), BF)
    return pl.pallas_call(
        pair_kernel,
        out_shape=(
            panel,
            panel,
            panel,
            jax.ShapeDtypeStruct((upper, hidden), BF),
            jax.ShapeDtypeStruct((2 * PANEL + upper, hidden), BF),
        ),
        in_specs=[pl.BlockSpec(memory_space=pltpu.SMEM)] * 2
        + [vmem]
        + [pl.BlockSpec(memory_space=pltpu.HBM)] * 4
        + [vmem] * 4,
        out_specs=(vmem,) * 5,
        scratch_shapes=[
            pltpu.SMEM((40,), jnp.int32),
            pltpu.VMEM((4, PANEL, hidden), BF),
            pltpu.SemaphoreType.DMA((4,)),
            pltpu.VMEM((PANEL, hidden), F32),
            pltpu.VMEM((4 * PANEL, hidden), F32),
            pltpu.VMEM((32, 8, tile), F32),
            pltpu.VMEM((hidden, upper), BF),
            pltpu.VMEM((tile, hidden), BF),
            pltpu.VMEM((tile, hidden), BF),
            pltpu.VMEM((PANEL, hidden), F32),
            pltpu.VMEM((4 * PANEL, hidden), F32),
            pltpu.VMEM((upper, hidden), F32),
            pltpu.VMEM((upper, 128), F32),
        ],
        compiler_params=pltpu.CompilerParams(vmem_limit_bytes=24 << 20),
        cost_estimate=pl.CostEstimate(
            flops=10 * 24 * tile * hidden * upper, bytes_accessed=2 << 20, transcendentals=24 * tile * hidden
        ),
        name="pair_grads",
    )(core, ids_s, ids, *[pltpu.with_memory_space_constraint(v, pltpu.HBM) for v in (left, right_o, right_m, right_p)], targets, bias, wmt, wf)


def send_kernel(blocks, live, targets_ref, out_ref, acc):
    tile = out_ref.shape[1]
    acc[...] = jnp.zeros_like(acc)
    lane = lax.broadcasted_iota(jnp.int32, (1, tile), 1)
    counters = (lane == 0) | (lane == PANEL + 1) | (lane == 2 * (PANEL + 1))

    def slot(i, carry):
        row = blocks[0, i]
        side = blocks[1, i] - row + 1
        to = row * 3 + side
        for rt in range(8):
            value = targets_ref[pl.ds(i, 1), rt * tile : (rt + 1) * tile]
            if rt == 0:
                value = jnp.where(counters & (side == 1), 0.0, value)
            acc[to, rt : rt + 1, :] += value
        acc[row * 3 + 1, 0:1, :] += jnp.where(lane == side * (PANEL + 1), 1.0, 0.0)
        return carry

    lax.fori_loop(0, live[0, 0], slot, 0)
    for p in range(acc.shape[0]):
        out_ref[p * 8 : (p + 1) * 8, :] = acc[p].astype(BF)


def send_targets(blocks, live, targets, panels):
    tile = ROWS * PANEL
    smem = pl.BlockSpec(memory_space=pltpu.SMEM)
    vmem = pl.BlockSpec(memory_space=pltpu.VMEM)
    return pl.pallas_call(
        send_kernel,
        out_shape=jax.ShapeDtypeStruct((24 * panels, tile), BF),
        in_specs=[smem, smem, vmem],
        out_specs=vmem,
        scratch_shapes=[pltpu.VMEM((3 * panels, 8, tile), F32)],
        compiler_params=pltpu.CompilerParams(vmem_limit_bytes=8 << 20),
        name="send_targets",
    )(blocks, live, targets)


def slice_kernel(*refs):
    embs, parts, out, emb_s, part_s = refs[:8], refs[8:12], refs[12], refs[13], refs[14]
    rows, depth = embs[0].shape
    for n, ref in enumerate(embs):
        emb_s[n * rows : (n + 1) * rows, :] = ref[...]
    for n, ref in enumerate(parts):
        part_s[n * 2 * rows : (n + 1) * 2 * rows, :] = ref[0 : 2 * rows, :]
    out[0:depth, :] = lax.dot_general(
        emb_s[...], part_s[...], (((0,), (0,)), ((), ())), preferred_element_type=F32
    ).astype(BF)
    out[depth:, :] = sum(ref[2 * rows :, :].astype(F32) for ref in parts).astype(BF)


def weight_slice(embs, parts):
    rows, depth = embs[0].shape
    width = parts[0].shape[1]
    vmem = pl.BlockSpec(memory_space=pltpu.VMEM)
    return pl.pallas_call(
        slice_kernel,
        out_shape=jax.ShapeDtypeStruct((depth + parts[0].shape[0] - 2 * rows, width), BF),
        in_specs=[vmem] * 12,
        out_specs=vmem,
        scratch_shapes=[pltpu.VMEM((8 * rows, depth), BF), pltpu.VMEM((8 * rows, width), BF)],
        compiler_params=pltpu.CompilerParams(vmem_limit_bytes=16 << 20),
        name="weight_slice",
    )(*embs, *parts)


ORDER = (0, 1, 3, 2)


def finish_kernel(scale, pos, *refs):
    pieces, (left_ref, right_ref, mid_ref, bias_ref, fin_ref, whole) = refs[:8], refs[8:]
    part = whole.shape[2] // 4
    depth = whole.shape[2] - 128
    block = left_ref.shape[0]

    @pl.when(pl.program_id(0) == 0)
    def _():
        for n, ref in enumerate(pieces):
            side = pos[0] if n < 4 else 1 - pos[0]
            column = lax.rem(pos[1] - ORDER[n % 4] + 4, 4)
            for m, dy in enumerate(ORDER):
                row = pl.multiple_of(lax.rem(pos[2] - dy + 4, 4) * part, 32)
                whole[side, column, pl.ds(row, part), :] = ref[m * part : (m + 1) * part, :]
        for j in range(4):
            lanes = slice(j * 128, (j + 1) * 128)
            mid_ref[lanes, :] = whole[0, j, depth : depth + 128, :].astype(F32) * scale
            bias_ref[:, lanes] = whole[1, j, depth : depth + 1, :].astype(F32) * scale
        fin_ref[...] = whole[1, 0, depth + 16 : depth + 17, :].astype(F32) * scale

    rows = pl.ds(pl.multiple_of(pl.program_id(0) * block, block), block)
    for j in range(4):
        lanes = slice(j * 128, (j + 1) * 128)
        left_ref[:, lanes] = whole[0, j, rows, :].astype(F32) * scale
        right_ref[:, lanes] = whole[1, j, rows, :].astype(F32) * scale


def local(
    embeddings,
    cluster_ids,
    block_list,
    block_counts,
    pair_targets,
    w_left,
    w_right,
    hidden_bias,
    w_middle,
    w_final,
):
    emb = embeddings[0]
    depth = emb.shape[1]
    hidden = w_left.shape[1]
    upper = w_middle.shape[1]
    panels = lax.axis_size("blk")
    groups = lax.axis_size("grp")
    me = lax.axis_index("blk")
    core, x, y = me & 1, (me >> 1) & 3, me >> 3

    def blk(value, partner):
        return lax.ppermute(value, "blk", [(i, partner(i)) for i in range(panels)])

    def on_core(value):
        return blk(value, lambda i: i ^ 1)

    def on_outer(value):
        return blk(value, lambda i: (i - 1 if i % 2 == 0 else i + 1) % panels)

    def on_x(value, d):
        return blk(value, lambda i: i // 8 * 8 + (i // 2 % 4 + d) % 4 * 2 + i % 2)

    def on_y(value, d):
        return blk(value, lambda i: (i // 8 + d) % 4 * 8 + i % 8)

    def on_z(value, d):
        return lax.ppermute(value, "grp", [(i, (i + d) % groups) for i in range(groups)])

    sums = send_targets(block_list[0].T, block_counts, pair_targets[0], panels).reshape(panels, 24, ROWS * PANEL)
    targets = lax.all_to_all(sums, "blk", 0, 0, tiled=True)
    targets = targets.reshape(24 * panels, ROWS * PANEL)

    right = jnp.dot(emb, w_right, preferred_element_type=F32).astype(BF)
    ids = cluster_ids[0].astype(BF)
    ids_row = jnp.pad(ids[None, :], ((0, 15), (0, hidden - PANEL)))
    right_own = jnp.concatenate([right, ids_row], axis=0)
    right_outer = on_outer(right_own)
    right_partner = on_core(right_own)

    left = jnp.dot(emb, w_left, preferred_element_type=F32).astype(BF)
    outer_ids = right_outer[PANEL, :PANEL]
    partner_ids = right_partner[PANEL, :PANEL]
    before = jnp.where(me == 0, BF(-1), jnp.where(core == 0, outer_ids, partner_ids))
    after = jnp.where(me == panels - 1, BF(127), jnp.where(core == 0, partner_ids, outer_ids))
    col_ids = jnp.stack([before, ids, after])

    embs = [emb]
    for d in ORDER[1:]:
        embs.append(on_x(emb, d))

    lg, r_outer, r_own, keep, sent = pair_grads(
        core[None],
        col_ids.astype(jnp.int32),
        jnp.pad(col_ids.astype(F32), ((0, 5), (0, 0))),
        left,
        right_outer,
        right_own,
        right_partner,
        targets,
        hidden_bias[None, :],
        w_middle.T,
        w_final[:, None],
    )

    first = core == 0
    got = on_core(sent)
    over = lax.ppermute(r_outer, "blk", [(i, (i + 2) % panels) for i in range(1, panels, 2)]).astype(F32)
    outer = on_outer(r_outer).astype(F32)
    chip = []
    for piece in embs:
        chip += [piece, on_core(piece)]
    r_partner = sent[PANEL : 2 * PANEL].astype(F32)
    rg = (r_own.astype(F32) + got[PANEL : 2 * PANEL].astype(F32) + outer).astype(BF)
    pair_right = (got[:PANEL].astype(F32) + r_partner + over).astype(BF)
    extra = keep.astype(F32) + got[2 * PANEL :].astype(F32)
    both = jnp.concatenate(
        [jnp.where(first, lg, rg), jnp.where(first, got[:PANEL], pair_right), extra.astype(BF)], axis=0
    )
    grad_local = jnp.dot(lg, w_left.T, preferred_element_type=F32) + jnp.dot(
        rg, w_right.T, preferred_element_type=F32
    )

    def column(d):
        return lax.dynamic_slice_in_dim(both, ((x + d) & 3) * 128, 128, 1)

    parts = [column(0)]
    for d in ORDER[1:]:
        parts.append(on_x(column(d), d))
    total = weight_slice(chip, parts)
    piece = total.shape[0] // 4

    def rows(d):
        return lax.dynamic_slice_in_dim(total, ((y + d) & 3) * piece, piece, 0)

    parts = [rows(0)] + [on_y(rows(d), d) for d in ORDER[1:]]
    total = sum(p.astype(F32) for p in parts).astype(BF)
    total = (
        total.astype(F32)
        + lax.ppermute(total, "grp", [(i, i ^ 1) for i in range(groups)]).astype(F32)
    ).astype(BF)
    total = sum(p.astype(F32) for p in [total] + [on_z(total, d) for d in (2, 6, 4)]).astype(BF)
    total, grad_local = lax.optimization_barrier((total, grad_local))

    total = jnp.concatenate([total] + [on_y(total, d) for d in ORDER[1:]], axis=0)
    mine = [total] + [on_x(total, d) for d in ORDER[1:]]
    theirs = [on_core(p) for p in mine]
    devices = panels * groups
    scale = 1.0 / math.sqrt(devices * B_DEV * PANEL)
    vmem = pl.BlockSpec(memory_space=pltpu.VMEM)
    block = depth // 4
    grad_left, grad_right, grad_middle, grad_bias, grad_final = pl.pallas_call(
        lambda *refs: finish_kernel(scale, *refs),
        grid=(4,),
        out_shape=(
            jax.ShapeDtypeStruct((depth, hidden), F32),
            jax.ShapeDtypeStruct((depth, hidden), F32),
            jax.ShapeDtypeStruct((hidden, upper), F32),
            jax.ShapeDtypeStruct((1, hidden), F32),
            jax.ShapeDtypeStruct((1, upper), F32),
        ),
        in_specs=[pl.BlockSpec(memory_space=pltpu.SMEM)] + [vmem] * 8,
        out_specs=(
            pl.BlockSpec((block, hidden), lambda i: (i, 0)),
            pl.BlockSpec((block, hidden), lambda i: (i, 0)),
            pl.BlockSpec((hidden, upper), lambda i: (0, 0)),
            pl.BlockSpec((1, hidden), lambda i: (0, 0)),
            pl.BlockSpec((1, upper), lambda i: (0, 0)),
        ),
        scratch_shapes=[pltpu.VMEM((2, 4, 4 * piece, 128), BF)],
        compiler_params=pltpu.CompilerParams(vmem_limit_bytes=16 << 20),
        name="finish",
    )(jnp.stack([core, x, y]), *mine, *theirs)
    return (grad_local[None], grad_left, grad_right, grad_bias[0], grad_middle, grad_final[0])


def solution(mesh):
    return jax.shard_map(
        local,
        mesh=mesh,
        in_specs=(
            P("grp", "blk", None),
            P("grp", "blk"),
            P("grp", "blk", None),
            P("grp", "blk"),
            P("grp", "blk", None),
            P(),
            P(),
            P(),
            P(),
            P(),
        ),
        out_specs=(P("grp", "blk", None), P(), P(), P(), P(), P()),
        check_vma=False,
    )
```

profile of v0, /device:TPU:1, one launch (start us, length us, event | category | flops | bytes accessed | tf_op | source)
XLA Modules:
  0.0 116.6 jit_solution(16586001091814499800)
XLA Ops:
  3.0 1.6 %send_targets.1 = bf16[768,512]{1,0:T(8,128)(2,1)} custom-call(s32[2,8]{1,0:T(2,128)S(1)} %bitcast.33, s32[1,1]{1,0:T(1,128)S(6)} %copy.21.live, f32[8,4096]{1,0:T(8,128)S(1)} %bitcast.32), custom_call_target="tpu_custom_call" | custom-call | tf_op jit(solution)/shard_map/send_targets/pallas_call | solution.py:286
  4.6 8.8 %all-to-all-start = ((bf16[32,24,512]{2,1,0:T(8,128)(2,1)}), bf16[32,24,512]{2,1,0:T(8,128)(2,1)S(1)}, u32[]{:S(2)}, u32[]{:S(2)}) async-start(bf16[32,24,512]{2,1,0:T(8,128)(2,1)} %bitcast.5), calls=%async_computation | async-start | bytes 1572864 | tf_op jit(solution)/shard_map/all_to_all | solution.py:395
  15.6 2.1 %convolution_convert_fusion.left_ref = bf16[64,512]{1,0:T(8,128)(2,1)} fusion(bf16[1024,512]{1,0:T(8,128)(2,1)} %param.15, bf16[1,64,1024]{2,1,0:T(8,128)(2,1)S(1)} %copy-done.1), kind=kOutput, calls=%fused_computation.1 | convolution fusion | flops 67141632 | bytes 1245184 | tf_op jit(solution)/shard_map/dot_general | solution.py:405
  18.0 7.4 %collective-permute-done.7.right_o = bf16[80,512]{1,0:T(8,128)(2,1)S(1)} collective-permute-done((bf16[80,512]{1,0:T(8,128)(2,1)S(1)}, bf16[80,512]{1,0:T(8,128)(2,1)S(1)}, u32[]{:S(2)}, u32[]{:S(2)}) %collective-permute-start.7) | collective-permute-done | bytes 81952 | tf_op jit(solution)/shard_map/ppermute | solution.py:377
  25.4 2.9 %all-to-all-done = bf16[32,24,512]{2,1,0:T(8,128)(2,1)S(1)} async-done(((bf16[32,24,512]{2,1,0:T(8,128)(2,1)}), bf16[32,24,512]{2,1,0:T(8,128)(2,1)S(1)}, u32[]{:S(2)}, u32[]{:S(2)}) %all-to-all-start) | async-done | bytes 786464 | tf_op jit(solution)/shard_map/all_to_all | solution.py:395
  28.3 12.9 %pair_grads.1 = (bf16[64,512]{1,0:T(8,128)(2,1)S(1)}, bf16[64,512]{1,0:T(8,128)(2,1)S(1)}, bf16[64,512]{1,0:T(8,128)(2,1)S(1)}, bf16[128,512]{1,0:T(8,128)(2,1)S(1)}, bf16[256,512]{1,0:T(8,128)(2,1)S(1)}) custom-call(s32[1]{0:T(128)} %bitcast.1.core, s32[3,64]{1,0:T(4,128)S(1)} %get-tuple-element.30.ids_s, f32[8,64]{1,0:T(8,128)S(1)} %pad_convert_fusion.ids_ref, ...), custom_call_target="tpu_custom_call" | custom-call | flops 8053063680 | bytes 2097152 | tf_op jit(solution)/shard_map/pair_grads/pallas_call | solution.py:222
  41.3 2.4 %collective-permute-start.9 = (bf16[256,512]{1,0:T(8,128)(2,1)S(1)}, bf16[256,512]{1,0:T(8,128)(2,1)S(1)}, u32[]{:S(2)}, u32[]{:S(2)}) collective-permute-start(bf16[256,512]{1,0:T(8,128)(2,1)S(1)} %get-tuple-element.20), channel_id=1, source_target_pairs={{0,1},{1,0},{2,3},{3,2},{4,5},{5,4},{6,7},{7,6},{8,9},{9,8},{10,11... | collective-permute-start | bytes 786440 | tf_op jit(solution)/shard_map/ppermute | solution.py:377
  46.2 2.2 %collective-permute-start.11 = (bf16[64,512]{1,0:T(8,128)(2,1)S(1)}, bf16[64,512]{1,0:T(8,128)(2,1)S(1)}, u32[]{:S(2)}, u32[]{:S(2)}) collective-permute-start(bf16[64,512]{1,0:T(8,128)(2,1)S(1)} %get-tuple-element.21), channel_id=1, source_target_pairs={{1,3},{3,5},{5,7},{7,9},{9,11},{11,13},{13,15},{15,17},{17,19},{19... | collective-permute-start | bytes 196616 | tf_op jit(solution)/shard_map/ppermute | solution.py:432
  50.1 3.5 %collective-permute-start = (bf16[64,1024]{1,0:T(8,128)(2,1)S(1)}, bf16[64,1024]{1,0:T(8,128)(2,1)S(1)}, u32[]{:S(2)}, u32[]{:S(2)}) collective-permute-start(bf16[64,1024]{1,0:T(8,128)(2,1)S(1)} %bitcast.28), channel_id=1, source_target_pairs={{0,1},{1,0},{2,3},{3,2},{4,5},{5,4},{6,7},{7,6},{8,9},{9,8},{10,11... | collective-permute-start | bytes 393224 | tf_op jit(solution)/shard_map/ppermute | solution.py:377
  55.4 1.7 %collective-permute-start.13 = (bf16[256,128]{1,0:T(8,128)(2,1)S(1)}, bf16[256,128]{1,0:T(8,128)(2,1)S(1)}, u32[]{:S(2)}, u32[]{:S(2)}) collective-permute-start(bf16[256,128]{1,0:T(8,128)(2,1)S(1)} %get-tuple-element.36), channel_id=1, source_target_pairs={{0,6},{1,7},{2,0},{3,1},{4,2},{5,3},{6,4},{7,5},{8,14},{9,15},{10,... | collective-permute-start | bytes 196616 | tf_op jit(solution)/shard_map/ppermute | solution.py:377
  57.0 2.4 %collective-permute-done.14.refs_11_ = bf16[256,128]{1,0:T(8,128)(2,1)S(1)} collective-permute-done((bf16[256,128]{1,0:T(8,128)(2,1)S(1)}, bf16[256,128]{1,0:T(8,128)(2,1)S(1)}, u32[]{:S(2)}, u32[]{:S(2)}) %collective-permute-start.14) | collective-permute-done | bytes 65568 | tf_op jit(solution)/shard_map/ppermute | solution.py:377
  59.4 2.6 %collective-permute-done.12.refs_9_ = bf16[256,128]{1,0:T(8,128)(2,1)S(1)} collective-permute-done((bf16[256,128]{1,0:T(8,128)(2,1)S(1)}, bf16[256,128]{1,0:T(8,128)(2,1)S(1)}, u32[]{:S(2)}, u32[]{:S(2)}) %collective-permute-start.12) | collective-permute-done | bytes 65568 | tf_op jit(solution)/shard_map/ppermute | solution.py:377
  63.7 3.9 %collective-permute-start.17 = (bf16[288,128]{1,0:T(8,128)(2,1)S(1)}, bf16[288,128]{1,0:T(8,128)(2,1)S(1)}, u32[]{:S(2)}, u32[]{:S(2)}) collective-permute-start(bf16[288,128]{1,0:T(8,128)(2,1)S(1)} %get-tuple-element.33), channel_id=1, source_target_pairs={{0,16},{1,17},{2,18},{3,19},{4,20},{5,21},{6,22},{7,23},{8,24},{9,... | collective-permute-start | bytes 221192 | tf_op jit(solution)/shard_map/ppermute | solution.py:377
  68.1 2.7 %collective-permute-done.17 = bf16[288,128]{1,0:T(8,128)(2,1)S(1)} collective-permute-done((bf16[288,128]{1,0:T(8,128)(2,1)S(1)}, bf16[288,128]{1,0:T(8,128)(2,1)S(1)}, u32[]{:S(2)}, u32[]{:S(2)}) %collective-permute-start.17) | collective-permute-done | bytes 73760 | tf_op jit(solution)/shard_map/ppermute | solution.py:377
  71.1 1.7 %collective-permute-start.18 = (bf16[288,128]{1,0:T(8,128)(2,1)S(1)}, bf16[288,128]{1,0:T(8,128)(2,1)S(1)}, u32[]{:S(2)}, u32[]{:S(2)}) collective-permute-start(bf16[288,128]{1,0:T(8,128)(2,1)S(1)} %add_convert_fusion.3), channel_id=1, source_target_pairs={{0,32},{32,0},{64,96},{96,64},{128,160},{160,128},{192,224},{224,1... | collective-permute-start | bytes 221192 | tf_op jit(solution)/shard_map/ppermute | solution.py:464
  74.6 7.3 %collective-permute-start.21 = (bf16[288,128]{1,0:T(8,128)(2,1)S(1)}, bf16[288,128]{1,0:T(8,128)(2,1)S(1)}, u32[]{:S(2)}, u32[]{:S(2)}) collective-permute-start(bf16[288,128]{1,0:T(8,128)(2,1)S(1)} %add_convert_fusion.2), channel_id=1, source_target_pairs={{0,128},{32,160},{64,192},{96,224},{128,0},{160,32},{192,64},{224,... | collective-permute-start | bytes 221192 | tf_op jit(solution)/shard_map/ppermute | solution.py:392
  81.9 2.4 %collective-permute-start.19 = (bf16[288,128]{1,0:T(8,128)(2,1)S(1)}, bf16[288,128]{1,0:T(8,128)(2,1)S(1)}, u32[]{:S(2)}, u32[]{:S(2)}) collective-permute-start(bf16[288,128]{1,0:T(8,128)(2,1)S(1)} %add_convert_fusion.2), channel_id=1, source_target_pairs={{0,64},{32,96},{64,128},{96,160},{128,192},{160,224},{192,0},{224,... | collective-permute-start | bytes 221192 | tf_op jit(solution)/shard_map/ppermute | solution.py:392
  84.3 2.4 %convolution_add_fusion = f32[64,1024]{1,0:T(8,128)} fusion(f32[64,1024]{1,0:T(8,128)S(1)} %fusion.5, bf16[64,512]{1,0:T(8,128)(2,1)S(1)} %get-tuple-element.18, bf16[1024,512]{1,0:T(8,128)(2,1)} %param.15), kind=kOutput, calls=%fused_computation | convolution fusion | flops 67174400 | bytes 1638400 | tf_op jit(solution)/shard_map/dot_general | solution.py:444
  87.8 1.6 %collective-permute-start.24 = (bf16[288,128]{1,0:T(8,128)(2,1)S(1)}, bf16[288,128]{1,0:T(8,128)(2,1)S(1)}, u32[]{:S(2)}, u32[]{:S(2)}) collective-permute-start(bf16[288,128]{1,0:T(8,128)(2,1)S(1)} %add_convert_fusion.1), channel_id=1, source_target_pairs={{0,16},{1,17},{2,18},{3,19},{4,20},{5,21},{6,22},{7,23},{8,24},{9,... | collective-permute-start | bytes 221192 | tf_op jit(solution)/shard_map/ppermute | solution.py:377
  90.8 3.8 %collective-permute-done.22 = bf16[288,128]{1,0:T(8,128)(2,1)S(1)} collective-permute-done((bf16[288,128]{1,0:T(8,128)(2,1)S(1)}, bf16[288,128]{1,0:T(8,128)(2,1)S(1)}, u32[]{:S(2)}, u32[]{:S(2)}) %collective-permute-start.22) | collective-permute-done | bytes 73760 | tf_op jit(solution)/shard_map/ppermute | solution.py:377
  97.1 6.9 %collective-permute-start.28 = (bf16[1152,128]{1,0:T(8,128)(2,1)S(1)}, bf16[1152,128]{1,0:T(8,128)(2,1)S(1)}, u32[]{:S(2)}, u32[]{:S(2)}) collective-permute-start(bf16[1152,128]{1,0:T(8,128)(2,1)S(1)} %constant_dynamic-update-slice_fusion.refs_1_), channel_id=1, source_target_pairs={{0,1},{1,0},{2,3},{3,2},{4,5},{5,4},{6,7},{7,6},{8,9},{9,8},{10,11... | collective-permute-start | bytes 884744 | tf_op jit(solution)/shard_map/ppermute | solution.py:377
  104.1 4.9 %collective-permute-start.31 = (bf16[1152,128]{1,0:T(8,128)(2,1)S(1)}, bf16[1152,128]{1,0:T(8,128)(2,1)S(1)}, u32[]{:S(2)}, u32[]{:S(2)}) collective-permute-start(bf16[1152,128]{1,0:T(8,128)(2,1)S(1)} %collective-permute-done.27.refs_4_), channel_id=1, source_target_pairs={{0,1},{1,0},{2,3},{3,2},{4,5},{5,4},{6,7},{7,6},{8,9},{9,8},{10,11... | collective-permute-start | bytes 884744 | tf_op jit(solution)/shard_map/ppermute | solution.py:377
  109.0 1.6 %collective-permute-start.30 = (bf16[1152,128]{1,0:T(8,128)(2,1)S(1)}, bf16[1152,128]{1,0:T(8,128)(2,1)S(1)}, u32[]{:S(2)}, u32[]{:S(2)}) collective-permute-start(bf16[1152,128]{1,0:T(8,128)(2,1)S(1)} %collective-permute-done.26.refs_3_), channel_id=1, source_target_pairs={{0,1},{1,0},{2,3},{3,2},{4,5},{5,4},{6,7},{7,6},{8,9},{9,8},{10,11... | collective-permute-start | bytes 884744 | tf_op jit(solution)/shard_map/ppermute | solution.py:377
  113.2 3.4 %finish.1 = (f32[1024,512]{1,0:T(8,128)}, f32[1024,512]{1,0:T(8,128)}, f32[512,128]{1,0:T(8,128)}, f32[1,512]{1,0:T(1,128)}, f32[1,128]{1,0:T(1,128)}) custom-call(s32[3]{0:T(128)S(1)} %pad_add_fusion.refs_0_, bf16[1152,128]{1,0:T(8,128)(2,1)S(1)} %constant_dynamic-update-slice_fusion.refs_1_, bf16[1152,128]{1,0:T(8,128)(2,1)S(1)} %collective-permute-done.25.refs_2_, ...), custom_call_target="tpu_custom_call" | custom-call | tf_op jit(solution)/shard_map/finish/pallas_call | solution.py:476
  (92 shorter events, 22.0 us)
Async XLA Ops:
  4.6 23.7 %all-to-all-start = ((bf16[32,24,512]{2,1,0:T(8,128)(2,1)}), bf16[32,24,512]{2,1,0:T(8,128)(2,1)S(1)}, u32[]{:S(2)}, u32[]{:S(2)}) async-start(bf16[32,24,512]{2,1,0:T(8,128)(2,1)} %bitcast.5), calls=%async_computation | async-start | bytes 1572864 | tf_op jit(solution)/shard_map/all_to_all | solution.py:395
  14.1 11.3 %collective-permute-start.7 = (bf16[80,512]{1,0:T(8,128)(2,1)S(1)}, bf16[80,512]{1,0:T(8,128)(2,1)S(1)}, u32[]{:S(2)}, u32[]{:S(2)}) collective-permute-start(bf16[80,512]{1,0:T(8,128)(2,1)S(1)} %fusion.2.right_m), channel_id=1, source_target_pairs={{0,31},{1,2},{2,1},{3,4},{4,3},{5,6},{6,5},{7,8},{8,7},{9,10},{10,... | collective-permute-start | bytes 245768 | tf_op jit(solution)/shard_map/ppermute | solution.py:377
  41.3 7.1 %collective-permute-start.9 = (bf16[256,512]{1,0:T(8,128)(2,1)S(1)}, bf16[256,512]{1,0:T(8,128)(2,1)S(1)}, u32[]{:S(2)}, u32[]{:S(2)}) collective-permute-start(bf16[256,512]{1,0:T(8,128)(2,1)S(1)} %get-tuple-element.20), channel_id=1, source_target_pairs={{0,1},{1,0},{2,3},{3,2},{4,5},{5,4},{6,7},{7,6},{8,9},{9,8},{10,11... | collective-permute-start | bytes 786440 | tf_op jit(solution)/shard_map/ppermute | solution.py:377
  43.6 6.5 %collective-permute-start.5 = (bf16[64,1024]{1,0:T(8,128)(2,1)S(1)}, bf16[64,1024]{1,0:T(8,128)(2,1)S(1)}, u32[]{:S(2)}, u32[]{:S(2)}) collective-permute-start(bf16[64,1024]{1,0:T(8,128)(2,1)S(1)} %bitcast.25), channel_id=1, source_target_pairs={{0,4},{1,5},{2,6},{3,7},{4,0},{5,1},{6,2},{7,3},{8,12},{9,13},{10,... | collective-permute-start | bytes 393224 | tf_op jit(solution)/shard_map/ppermute | solution.py:377
  44.8 8.8 %collective-permute-start.3 = (bf16[64,1024]{1,0:T(8,128)(2,1)S(1)}, bf16[64,1024]{1,0:T(8,128)(2,1)S(1)}, u32[]{:S(2)}, u32[]{:S(2)}) collective-permute-start(bf16[64,1024]{1,0:T(8,128)(2,1)S(1)} %bitcast.26), channel_id=1, source_target_pairs={{0,6},{1,7},{2,0},{3,1},{4,2},{5,3},{6,4},{7,5},{8,14},{9,15},{10,... | collective-permute-start | bytes 393224 | tf_op jit(solution)/shard_map/ppermute | solution.py:377
  44.8 8.9 %collective-permute-start.1 = (bf16[64,1024]{1,0:T(8,128)(2,1)S(1)}, bf16[64,1024]{1,0:T(8,128)(2,1)S(1)}, u32[]{:S(2)}, u32[]{:S(2)}) collective-permute-start(bf16[64,1024]{1,0:T(8,128)(2,1)S(1)} %bitcast.27), channel_id=1, source_target_pairs={{0,2},{1,3},{2,4},{3,5},{4,6},{5,7},{6,0},{7,1},{8,10},{9,11},{10,... | collective-permute-start | bytes 393224 | tf_op jit(solution)/shard_map/ppermute | solution.py:377
  46.2 8.3 %collective-permute-start.11 = (bf16[64,512]{1,0:T(8,128)(2,1)S(1)}, bf16[64,512]{1,0:T(8,128)(2,1)S(1)}, u32[]{:S(2)}, u32[]{:S(2)}) collective-permute-start(bf16[64,512]{1,0:T(8,128)(2,1)S(1)} %get-tuple-element.21), channel_id=1, source_target_pairs={{1,3},{3,5},{5,7},{7,9},{9,11},{11,13},{13,15},{15,17},{17,19},{19... | collective-permute-start | bytes 196616 | tf_op jit(solution)/shard_map/ppermute | solution.py:432
  48.4 6.2 %collective-permute-start.10 = (bf16[64,512]{1,0:T(8,128)(2,1)S(1)}, bf16[64,512]{1,0:T(8,128)(2,1)S(1)}, u32[]{:S(2)}, u32[]{:S(2)}) collective-permute-start(bf16[64,512]{1,0:T(8,128)(2,1)S(1)} %get-tuple-element.21), channel_id=1, source_target_pairs={{0,31},{1,2},{2,1},{3,4},{4,3},{5,6},{6,5},{7,8},{8,7},{9,10},{10,... | collective-permute-start | bytes 196616 | tf_op jit(solution)/shard_map/ppermute | solution.py:377
  50.1 5.3 %collective-permute-start = (bf16[64,1024]{1,0:T(8,128)(2,1)S(1)}, bf16[64,1024]{1,0:T(8,128)(2,1)S(1)}, u32[]{:S(2)}, u32[]{:S(2)}) collective-permute-start(bf16[64,1024]{1,0:T(8,128)(2,1)S(1)} %bitcast.28), channel_id=1, source_target_pairs={{0,1},{1,0},{2,3},{3,2},{4,5},{5,4},{6,7},{7,6},{8,9},{9,8},{10,11... | collective-permute-start | bytes 393224 | tf_op jit(solution)/shard_map/ppermute | solution.py:377
  54.7 4.7 %collective-permute-start.14 = (bf16[256,128]{1,0:T(8,128)(2,1)S(1)}, bf16[256,128]{1,0:T(8,128)(2,1)S(1)}, u32[]{:S(2)}, u32[]{:S(2)}) collective-permute-start(bf16[256,128]{1,0:T(8,128)(2,1)S(1)} %get-tuple-element.35), channel_id=1, source_target_pairs={{0,4},{1,5},{2,6},{3,7},{4,0},{5,1},{6,2},{7,3},{8,12},{9,13},{10,... | collective-permute-start | bytes 196616 | tf_op jit(solution)/shard_map/ppermute | solution.py:377
  57.0 5.0 %collective-permute-start.12 = (bf16[256,128]{1,0:T(8,128)(2,1)S(1)}, bf16[256,128]{1,0:T(8,128)(2,1)S(1)}, u32[]{:S(2)}, u32[]{:S(2)}) collective-permute-start(bf16[256,128]{1,0:T(8,128)(2,1)S(1)} %get-tuple-element.37), channel_id=1, source_target_pairs={{0,2},{1,3},{2,4},{3,5},{4,6},{5,7},{6,0},{7,1},{8,10},{9,11},{10,... | collective-permute-start | bytes 196616 | tf_op jit(solution)/shard_map/ppermute | solution.py:377
  62.6 5.6 %collective-permute-start.15 = (bf16[288,128]{1,0:T(8,128)(2,1)S(1)}, bf16[288,128]{1,0:T(8,128)(2,1)S(1)}, u32[]{:S(2)}, u32[]{:S(2)}) collective-permute-start(bf16[288,128]{1,0:T(8,128)(2,1)S(1)} %get-tuple-element.32), channel_id=1, source_target_pairs={{0,8},{1,9},{2,10},{3,11},{4,12},{5,13},{6,14},{7,15},{8,16},{9,17... | collective-permute-start | bytes 221192 | tf_op jit(solution)/shard_map/ppermute | solution.py:377
  63.7 7.2 %collective-permute-start.17 = (bf16[288,128]{1,0:T(8,128)(2,1)S(1)}, bf16[288,128]{1,0:T(8,128)(2,1)S(1)}, u32[]{:S(2)}, u32[]{:S(2)}) collective-permute-start(bf16[288,128]{1,0:T(8,128)(2,1)S(1)} %get-tuple-element.33), channel_id=1, source_target_pairs={{0,16},{1,17},{2,18},{3,19},{4,20},{5,21},{6,22},{7,23},{8,24},{9,... | collective-permute-start | bytes 221192 | tf_op jit(solution)/shard_map/ppermute | solution.py:377
  74.6 12.1 %collective-permute-start.21 = (bf16[288,128]{1,0:T(8,128)(2,1)S(1)}, bf16[288,128]{1,0:T(8,128)(2,1)S(1)}, u32[]{:S(2)}, u32[]{:S(2)}) collective-permute-start(bf16[288,128]{1,0:T(8,128)(2,1)S(1)} %add_convert_fusion.2), channel_id=1, source_target_pairs={{0,128},{32,160},{64,192},{96,224},{128,0},{160,32},{192,64},{224,... | collective-permute-start | bytes 221192 | tf_op jit(solution)/shard_map/ppermute | solution.py:392
  81.9 5.7 %collective-permute-start.20 = (bf16[288,128]{1,0:T(8,128)(2,1)S(1)}, bf16[288,128]{1,0:T(8,128)(2,1)S(1)}, u32[]{:S(2)}, u32[]{:S(2)}) collective-permute-start(bf16[288,128]{1,0:T(8,128)(2,1)S(1)} %add_convert_fusion.2), channel_id=1, source_target_pairs={{0,192},{32,224},{64,0},{96,32},{128,64},{160,96},{192,128},{224,1... | collective-permute-start | bytes 221192 | tf_op jit(solution)/shard_map/ppermute | solution.py:392
  81.9 5.8 %collective-permute-start.19 = (bf16[288,128]{1,0:T(8,128)(2,1)S(1)}, bf16[288,128]{1,0:T(8,128)(2,1)S(1)}, u32[]{:S(2)}, u32[]{:S(2)}) collective-permute-start(bf16[288,128]{1,0:T(8,128)(2,1)S(1)} %add_convert_fusion.2), channel_id=1, source_target_pairs={{0,64},{32,96},{64,128},{96,160},{128,192},{160,224},{192,0},{224,... | collective-permute-start | bytes 221192 | tf_op jit(solution)/shard_map/ppermute | solution.py:392
  87.8 6.9 %collective-permute-start.24 = (bf16[288,128]{1,0:T(8,128)(2,1)S(1)}, bf16[288,128]{1,0:T(8,128)(2,1)S(1)}, u32[]{:S(2)}, u32[]{:S(2)}) collective-permute-start(bf16[288,128]{1,0:T(8,128)(2,1)S(1)} %add_convert_fusion.1), channel_id=1, source_target_pairs={{0,16},{1,17},{2,18},{3,19},{4,20},{5,21},{6,22},{7,23},{8,24},{9,... | collective-permute-start | bytes 221192 | tf_op jit(solution)/shard_map/ppermute | solution.py:377
  89.3 5.3 %collective-permute-start.23 = (bf16[288,128]{1,0:T(8,128)(2,1)S(1)}, bf16[288,128]{1,0:T(8,128)(2,1)S(1)}, u32[]{:S(2)}, u32[]{:S(2)}) collective-permute-start(bf16[288,128]{1,0:T(8,128)(2,1)S(1)} %add_convert_fusion.1), channel_id=1, source_target_pairs={{0,24},{1,25},{2,26},{3,27},{4,28},{5,29},{6,30},{7,31},{8,0},{9,1... | collective-permute-start | bytes 221192 | tf_op jit(solution)/shard_map/ppermute | solution.py:377
  90.2 4.4 %collective-permute-start.22 = (bf16[288,128]{1,0:T(8,128)(2,1)S(1)}, bf16[288,128]{1,0:T(8,128)(2,1)S(1)}, u32[]{:S(2)}, u32[]{:S(2)}) collective-permute-start(bf16[288,128]{1,0:T(8,128)(2,1)S(1)} %add_convert_fusion.1), channel_id=1, source_target_pairs={{0,8},{1,9},{2,10},{3,11},{4,12},{5,13},{6,14},{7,15},{8,16},{9,17... | collective-permute-start | bytes 221192 | tf_op jit(solution)/shard_map/ppermute | solution.py:377
  94.7 9.4 %collective-permute-start.27 = (bf16[1152,128]{1,0:T(8,128)(2,1)S(1)}, bf16[1152,128]{1,0:T(8,128)(2,1)S(1)}, u32[]{:S(2)}, u32[]{:S(2)}) collective-permute-start(bf16[1152,128]{1,0:T(8,128)(2,1)S(1)} %constant_dynamic-update-slice_fusion.refs_1_), channel_id=1, source_target_pairs={{0,4},{1,5},{2,6},{3,7},{4,0},{5,1},{6,2},{7,3},{8,12},{9,13},{10,... | collective-permute-start | bytes 884744 | tf_op jit(solution)/shard_map/ppermute | solution.py:377
  95.7 13.3 %collective-permute-start.26 = (bf16[1152,128]{1,0:T(8,128)(2,1)S(1)}, bf16[1152,128]{1,0:T(8,128)(2,1)S(1)}, u32[]{:S(2)}, u32[]{:S(2)}) collective-permute-start(bf16[1152,128]{1,0:T(8,128)(2,1)S(1)} %constant_dynamic-update-slice_fusion.refs_1_), channel_id=1, source_target_pairs={{0,6},{1,7},{2,0},{3,1},{4,2},{5,3},{6,4},{7,5},{8,14},{9,15},{10,... | collective-permute-start | bytes 884744 | tf_op jit(solution)/shard_map/ppermute | solution.py:377
  96.8 13.8 %collective-permute-start.25 = (bf16[1152,128]{1,0:T(8,128)(2,1)S(1)}, bf16[1152,128]{1,0:T(8,128)(2,1)S(1)}, u32[]{:S(2)}, u32[]{:S(2)}) collective-permute-start(bf16[1152,128]{1,0:T(8,128)(2,1)S(1)} %constant_dynamic-update-slice_fusion.refs_1_), channel_id=1, source_target_pairs={{0,2},{1,3},{2,4},{3,5},{4,6},{5,7},{6,0},{7,1},{8,10},{9,11},{10,... | collective-permute-start | bytes 884744 | tf_op jit(solution)/shard_map/ppermute | solution.py:377
  97.1 15.0 %collective-permute-start.28 = (bf16[1152,128]{1,0:T(8,128)(2,1)S(1)}, bf16[1152,128]{1,0:T(8,128)(2,1)S(1)}, u32[]{:S(2)}, u32[]{:S(2)}) collective-permute-start(bf16[1152,128]{1,0:T(8,128)(2,1)S(1)} %constant_dynamic-update-slice_fusion.refs_1_), channel_id=1, source_target_pairs={{0,1},{1,0},{2,3},{3,2},{4,5},{5,4},{6,7},{7,6},{8,9},{9,8},{10,11... | collective-permute-start | bytes 884744 | tf_op jit(solution)/shard_map/ppermute | solution.py:377
  104.1 8.0 %collective-permute-start.31 = (bf16[1152,128]{1,0:T(8,128)(2,1)S(1)}, bf16[1152,128]{1,0:T(8,128)(2,1)S(1)}, u32[]{:S(2)}, u32[]{:S(2)}) collective-permute-start(bf16[1152,128]{1,0:T(8,128)(2,1)S(1)} %collective-permute-done.27.refs_4_), channel_id=1, source_target_pairs={{0,1},{1,0},{2,3},{3,2},{4,5},{5,4},{6,7},{7,6},{8,9},{9,8},{10,11... | collective-permute-start | bytes 884744 | tf_op jit(solution)/shard_map/ppermute | solution.py:377
  (20 other events, 145.7 us)
where the time goes:
time: 117 us
  starting transfers between devices  60.8 us (52%)
  waiting for transfers between devices  28.1 us (24%)
  Pallas kernels  18.5 us (16%)
  matrix products  5.23 us (4%)
  local copies, waits for them, and re-layouts  1.99 us (2%)
  between operations  1.67 us (1%)
    ppermute x27, starting transfers between devices, blk(): return lax.ppermute(value, 'blk', [(i, partner(i)) for i in range(panels)])  38.5 us
    ppermute x27, waiting for transfers between devices, blk(): return lax.ppermute(value, 'blk', [(i, partner(i)) for i in range(panels)])  22.4 us
    pallas_call x1, Pallas kernels, pair_grads(): pl.pallas_call(pair_kernel, out_shape=(panel, panel, panel, jax.ShapeDtyp...  12.9 us
    ppermute x3, starting transfers between devices, on_z(): lax.ppermute(value, 'grp', [(i, (i + d) % groups) for i in range(groups)])  9.69 us
    all_to_all x1, starting transfers between devices, local(): targets = lax.all_to_all(sums, 'blk', 0, 0, tiled=True)  8.76 us
    pallas_call x1, Pallas kernels, local(): pl.pallas_call(lambda *refs: finish_kernel(scale, *refs), grid=(4,), out_...  3.38 us
    all_to_all x1, waiting for transfers between devices, local(): targets = lax.all_to_all(sums, 'blk', 0, 0, tiled=True)  2.87 us
    dot_general x1, matrix products, local(): jnp.dot(lg, w_left.T, preferred_element_type=F32)  2.37 us
  transfers between devices with their start and end apart: 33, of which 14 were waited for; matrix products, arithmetic and copies ran while one was open for 5% of the time, Pallas kernels for 0%

commit v1 on v0

--- a/solution.py
+++ b/solution.py
@@ -256,9 +256,12 @@
     )(core, ids_s, ids, *[pltpu.with_memory_space_constraint(v, pltpu.HBM) for v in (left, right_o, right_m, right_p)], targets, bias, wmt, wf)
 
 
-def send_kernel(blocks, live, targets_ref, out_ref, acc):
+def send_kernel(blocks, live, targets_hbm, out_ref, acc, targets_ref, sem):
     tile = out_ref.shape[1]
+    load = pltpu.make_async_copy(targets_hbm, targets_ref, sem)
+    load.start()
     acc[...] = jnp.zeros_like(acc)
+    load.wait()
     lane = lax.broadcasted_iota(jnp.int32, (1, tile), 1)
     counters = (lane == 0) | (lane == PANEL + 1) | (lane == 2 * (PANEL + 1))
 
@@ -286,12 +289,16 @@
     return pl.pallas_call(
         send_kernel,
         out_shape=jax.ShapeDtypeStruct((24 * panels, tile), BF),
-        in_specs=[smem, smem, vmem],
+        in_specs=[smem, smem, pl.BlockSpec(memory_space=pltpu.HBM)],
         out_specs=vmem,
-        scratch_shapes=[pltpu.VMEM((3 * panels, 8, tile), F32)],
+        scratch_shapes=[
+            pltpu.VMEM((3 * panels, 8, tile), F32),
+            pltpu.VMEM(targets.shape, F32),
+            pltpu.SemaphoreType.DMA(()),
+        ],
         compiler_params=pltpu.CompilerParams(vmem_limit_bytes=8 << 20),
         name="send_targets",
-    )(blocks, live, targets)
+    )(blocks, live, pltpu.with_memory_space_constraint(targets, pltpu.HBM))
 
 
 def slice_kernel(*refs):

time: 117 us -> 117 us (level)
  no operation moved by 1% of the time
where the time goes in v1:
time: 117 us
  starting transfers between devices  60.7 us (52%)
  waiting for transfers between devices  28.2 us (24%)
  Pallas kernels  19.3 us (16%)
  matrix products  5.25 us (4%)
  between operations  1.7 us (1%)
    ppermute x27, starting transfers between devices, blk(): return lax.ppermute(value, 'blk', [(i, partner(i)) for i in range(panels)])  38.6 us
    ppermute x27, waiting for transfers between devices, blk(): return lax.ppermute(value, 'blk', [(i, partner(i)) for i in range(panels)])  22.5 us
    pallas_call x1, Pallas kernels, pair_grads(): pl.pallas_call(pair_kernel, out_shape=(panel, panel, panel, jax.ShapeDtyp...  13 us
    ppermute x3, starting transfers between devices, on_z(): lax.ppermute(value, 'grp', [(i, (i + d) % groups) for i in range(groups)])  9.78 us
    all_to_all x1, starting transfers between devices, local(): targets = lax.all_to_all(sums, 'blk', 0, 0, tiled=True)  8.77 us
    pallas_call x1, Pallas kernels, local(): pl.pallas_call(lambda *refs: finish_kernel(scale, *refs), grid=(4,), out_...  3.38 us
    all_to_all x1, waiting for transfers between devices, local(): targets = lax.all_to_all(sums, 'blk', 0, 0, tiled=True)  2.87 us
    pallas_call x1, Pallas kernels, send_targets(): pl.pallas_call(send_kernel, out_shape=jax.ShapeDtypeStruct((24 * panels,...  2.46 us
  transfers between devices with their start and end apart: 33, of which 14 were waited for; matrix products, arithmetic and copies ran while one was open for 5% of the time, Pallas kernels for 0%

profile of v1, /device:TPU:1, one launch (start us, length us, event | category | flops | bytes accessed | tf_op | source)
XLA Modules:
  0.0 116.7 jit_solution(10406195884515851637)
XLA Ops:
  2.1 2.5 %send_targets.1 = bf16[768,512]{1,0:T(8,128)(2,1)} custom-call(s32[2,8]{1,0:T(2,128)S(1)} %bitcast.32, s32[1,1]{1,0:T(1,128)S(6)} %copy.21.live, f32[8,4096]{1,0:T(8,128)} %bitcast.35), custom_call_target="tpu_custom_call" | custom-call | tf_op jit(solution)/shard_map/send_targets/pallas_call | solution.py:289
  4.6 8.8 %all-to-all-start = ((bf16[32,24,512]{2,1,0:T(8,128)(2,1)}), bf16[32,24,512]{2,1,0:T(8,128)(2,1)S(1)}, u32[]{:S(2)}, u32[]{:S(2)}) async-start(bf16[32,24,512]{2,1,0:T(8,128)(2,1)} %bitcast.5), calls=%async_computation | async-start | bytes 1572864 | tf_op jit(solution)/shard_map/all_to_all | solution.py:402
  15.6 2.2 %convolution_convert_fusion.left_ref = bf16[64,512]{1,0:T(8,128)(2,1)} fusion(bf16[1024,512]{1,0:T(8,128)(2,1)} %param.15, bf16[1,64,1024]{2,1,0:T(8,128)(2,1)S(1)} %copy-done.1), kind=kOutput, calls=%fused_computation.1 | convolution fusion | flops 67141632 | bytes 1245184 | tf_op jit(solution)/shard_map/dot_general | solution.py:412
  18.0 7.4 %collective-permute-done.7.right_o = bf16[80,512]{1,0:T(8,128)(2,1)S(1)} collective-permute-done((bf16[80,512]{1,0:T(8,128)(2,1)S(1)}, bf16[80,512]{1,0:T(8,128)(2,1)S(1)}, u32[]{:S(2)}, u32[]{:S(2)}) %collective-permute-start.7) | collective-permute-done | bytes 81952 | tf_op jit(solution)/shard_map/ppermute | solution.py:384
  25.4 2.9 %all-to-all-done = bf16[32,24,512]{2,1,0:T(8,128)(2,1)S(1)} async-done(((bf16[32,24,512]{2,1,0:T(8,128)(2,1)}), bf16[32,24,512]{2,1,0:T(8,128)(2,1)S(1)}, u32[]{:S(2)}, u32[]{:S(2)}) %all-to-all-start) | async-done | bytes 786464 | tf_op jit(solution)/shard_map/all_to_all | solution.py:402
  28.3 13.0 %pair_grads.1 = (bf16[64,512]{1,0:T(8,128)(2,1)S(1)}, bf16[64,512]{1,0:T(8,128)(2,1)S(1)}, bf16[64,512]{1,0:T(8,128)(2,1)S(1)}, bf16[128,512]{1,0:T(8,128)(2,1)S(1)}, bf16[256,512]{1,0:T(8,128)(2,1)S(1)}) custom-call(s32[1]{0:T(128)} %bitcast.1.core, s32[3,64]{1,0:T(4,128)S(1)} %get-tuple-element.30.ids_s, f32[8,64]{1,0:T(8,128)S(1)} %pad_convert_fusion.ids_ref, ...), custom_call_target="tpu_custom_call" | custom-call | flops 8053063680 | bytes 2097152 | tf_op jit(solution)/shard_map/pair_grads/pallas_call | solution.py:222
  41.3 2.3 %collective-permute-start.9 = (bf16[256,512]{1,0:T(8,128)(2,1)S(1)}, bf16[256,512]{1,0:T(8,128)(2,1)S(1)}, u32[]{:S(2)}, u32[]{:S(2)}) collective-permute-start(bf16[256,512]{1,0:T(8,128)(2,1)S(1)} %get-tuple-element.20), channel_id=1, source_target_pairs={{0,1},{1,0},{2,3},{3,2},{4,5},{5,4},{6,7},{7,6},{8,9},{9,8},{10,11... | collective-permute-start | bytes 786440 | tf_op jit(solution)/shard_map/ppermute | solution.py:384
  46.2 2.1 %collective-permute-start.11 = (bf16[64,512]{1,0:T(8,128)(2,1)S(1)}, bf16[64,512]{1,0:T(8,128)(2,1)S(1)}, u32[]{:S(2)}, u32[]{:S(2)}) collective-permute-start(bf16[64,512]{1,0:T(8,128)(2,1)S(1)} %get-tuple-element.21), channel_id=1, source_target_pairs={{1,3},{3,5},{5,7},{7,9},{9,11},{11,13},{13,15},{15,17},{17,19},{19... | collective-permute-start | bytes 196616 | tf_op jit(solution)/shard_map/ppermute | solution.py:439
  48.5 1.5 %collective-permute-done.5.refs_6_ = bf16[64,1024]{1,0:T(8,128)(2,1)S(1)} collective-permute-done((bf16[64,1024]{1,0:T(8,128)(2,1)S(1)}, bf16[64,1024]{1,0:T(8,128)(2,1)S(1)}, u32[]{:S(2)}, u32[]{:S(2)}) %collective-permute-start.5) | collective-permute-done | bytes 131104 | tf_op jit(solution)/shard_map/ppermute | solution.py:384
  50.0 3.5 %collective-permute-start = (bf16[64,1024]{1,0:T(8,128)(2,1)S(1)}, bf16[64,1024]{1,0:T(8,128)(2,1)S(1)}, u32[]{:S(2)}, u32[]{:S(2)}) collective-permute-start(bf16[64,1024]{1,0:T(8,128)(2,1)S(1)} %bitcast.28), channel_id=1, source_target_pairs={{0,1},{1,0},{2,3},{3,2},{4,5},{5,4},{6,7},{7,6},{8,9},{9,8},{10,11... | collective-permute-start | bytes 393224 | tf_op jit(solution)/shard_map/ppermute | solution.py:384
  55.4 1.7 %collective-permute-start.13 = (bf16[256,128]{1,0:T(8,128)(2,1)S(1)}, bf16[256,128]{1,0:T(8,128)(2,1)S(1)}, u32[]{:S(2)}, u32[]{:S(2)}) collective-permute-start(bf16[256,128]{1,0:T(8,128)(2,1)S(1)} %get-tuple-element.36), channel_id=1, source_target_pairs={{0,6},{1,7},{2,0},{3,1},{4,2},{5,3},{6,4},{7,5},{8,14},{9,15},{10,... | collective-permute-start | bytes 196616 | tf_op jit(solution)/shard_map/ppermute | solution.py:384
  57.0 2.4 %collective-permute-done.14.refs_11_ = bf16[256,128]{1,0:T(8,128)(2,1)S(1)} collective-permute-done((bf16[256,128]{1,0:T(8,128)(2,1)S(1)}, bf16[256,128]{1,0:T(8,128)(2,1)S(1)}, u32[]{:S(2)}, u32[]{:S(2)}) %collective-permute-start.14) | collective-permute-done | bytes 65568 | tf_op jit(solution)/shard_map/ppermute | solution.py:384
  59.4 2.6 %collective-permute-done.12.refs_9_ = bf16[256,128]{1,0:T(8,128)(2,1)S(1)} collective-permute-done((bf16[256,128]{1,0:T(8,128)(2,1)S(1)}, bf16[256,128]{1,0:T(8,128)(2,1)S(1)}, u32[]{:S(2)}, u32[]{:S(2)}) %collective-permute-start.12) | collective-permute-done | bytes 65568 | tf_op jit(solution)/shard_map/ppermute | solution.py:384
  63.6 4.0 %collective-permute-start.17 = (bf16[288,128]{1,0:T(8,128)(2,1)S(1)}, bf16[288,128]{1,0:T(8,128)(2,1)S(1)}, u32[]{:S(2)}, u32[]{:S(2)}) collective-permute-start(bf16[288,128]{1,0:T(8,128)(2,1)S(1)} %get-tuple-element.33), channel_id=1, source_target_pairs={{0,16},{1,17},{2,18},{3,19},{4,20},{5,21},{6,22},{7,23},{8,24},{9,... | collective-permute-start | bytes 221192 | tf_op jit(solution)/shard_map/ppermute | solution.py:384
  68.1 2.7 %collective-permute-done.17 = bf16[288,128]{1,0:T(8,128)(2,1)S(1)} collective-permute-done((bf16[288,128]{1,0:T(8,128)(2,1)S(1)}, bf16[288,128]{1,0:T(8,128)(2,1)S(1)}, u32[]{:S(2)}, u32[]{:S(2)}) %collective-permute-start.17) | collective-permute-done | bytes 73760 | tf_op jit(solution)/shard_map/ppermute | solution.py:384
  74.4 7.4 %collective-permute-start.21 = (bf16[288,128]{1,0:T(8,128)(2,1)S(1)}, bf16[288,128]{1,0:T(8,128)(2,1)S(1)}, u32[]{:S(2)}, u32[]{:S(2)}) collective-permute-start(bf16[288,128]{1,0:T(8,128)(2,1)S(1)} %add_convert_fusion.2), channel_id=1, source_target_pairs={{0,128},{32,160},{64,192},{96,224},{128,0},{160,32},{192,64},{224,... | collective-permute-start | bytes 221192 | tf_op jit(solution)/shard_map/ppermute | solution.py:399
  81.9 2.4 %collective-permute-start.19 = (bf16[288,128]{1,0:T(8,128)(2,1)S(1)}, bf16[288,128]{1,0:T(8,128)(2,1)S(1)}, u32[]{:S(2)}, u32[]{:S(2)}) collective-permute-start(bf16[288,128]{1,0:T(8,128)(2,1)S(1)} %add_convert_fusion.2), channel_id=1, source_target_pairs={{0,64},{32,96},{64,128},{96,160},{128,192},{160,224},{192,0},{224,... | collective-permute-start | bytes 221192 | tf_op jit(solution)/shard_map/ppermute | solution.py:399
  84.2 2.4 %convolution_add_fusion = f32[64,1024]{1,0:T(8,128)} fusion(f32[64,1024]{1,0:T(8,128)S(1)} %fusion.5, bf16[64,512]{1,0:T(8,128)(2,1)S(1)} %get-tuple-element.18, bf16[1024,512]{1,0:T(8,128)(2,1)} %param.15), kind=kOutput, calls=%fused_computation | convolution fusion | flops 67174400 | bytes 1638400 | tf_op jit(solution)/shard_map/dot_general | solution.py:451
  87.7 1.5 %collective-permute-start.24 = (bf16[288,128]{1,0:T(8,128)(2,1)S(1)}, bf16[288,128]{1,0:T(8,128)(2,1)S(1)}, u32[]{:S(2)}, u32[]{:S(2)}) collective-permute-start(bf16[288,128]{1,0:T(8,128)(2,1)S(1)} %add_convert_fusion.1), channel_id=1, source_target_pairs={{0,16},{1,17},{2,18},{3,19},{4,20},{5,21},{6,22},{7,23},{8,24},{9,... | collective-permute-start | bytes 221192 | tf_op jit(solution)/shard_map/ppermute | solution.py:384
  90.7 3.9 %collective-permute-done.22 = bf16[288,128]{1,0:T(8,128)(2,1)S(1)} collective-permute-done((bf16[288,128]{1,0:T(8,128)(2,1)S(1)}, bf16[288,128]{1,0:T(8,128)(2,1)S(1)}, u32[]{:S(2)}, u32[]{:S(2)}) %collective-permute-start.22) | collective-permute-done | bytes 73760 | tf_op jit(solution)/shard_map/ppermute | solution.py:384
  96.9 7.1 %collective-permute-start.28 = (bf16[1152,128]{1,0:T(8,128)(2,1)S(1)}, bf16[1152,128]{1,0:T(8,128)(2,1)S(1)}, u32[]{:S(2)}, u32[]{:S(2)}) collective-permute-start(bf16[1152,128]{1,0:T(8,128)(2,1)S(1)} %constant_dynamic-update-slice_fusion.refs_1_), channel_id=1, source_target_pairs={{0,1},{1,0},{2,3},{3,2},{4,5},{5,4},{6,7},{7,6},{8,9},{9,8},{10,11... | collective-permute-start | bytes 884744 | tf_op jit(solution)/shard_map/ppermute | solution.py:384
  104.0 5.0 %collective-permute-start.31 = (bf16[1152,128]{1,0:T(8,128)(2,1)S(1)}, bf16[1152,128]{1,0:T(8,128)(2,1)S(1)}, u32[]{:S(2)}, u32[]{:S(2)}) collective-permute-start(bf16[1152,128]{1,0:T(8,128)(2,1)S(1)} %collective-permute-done.27.refs_4_), channel_id=1, source_target_pairs={{0,1},{1,0},{2,3},{3,2},{4,5},{5,4},{6,7},{7,6},{8,9},{9,8},{10,11... | collective-permute-start | bytes 884744 | tf_op jit(solution)/shard_map/ppermute | solution.py:384
  109.0 1.6 %collective-permute-start.30 = (bf16[1152,128]{1,0:T(8,128)(2,1)S(1)}, bf16[1152,128]{1,0:T(8,128)(2,1)S(1)}, u32[]{:S(2)}, u32[]{:S(2)}) collective-permute-start(bf16[1152,128]{1,0:T(8,128)(2,1)S(1)} %collective-permute-done.26.refs_3_), channel_id=1, source_target_pairs={{0,1},{1,0},{2,3},{3,2},{4,5},{5,4},{6,7},{7,6},{8,9},{9,8},{10,11... | collective-permute-start | bytes 884744 | tf_op jit(solution)/shard_map/ppermute | solution.py:384
  113.3 3.4 %finish.1 = (f32[1024,512]{1,0:T(8,128)}, f32[1024,512]{1,0:T(8,128)}, f32[512,128]{1,0:T(8,128)}, f32[1,512]{1,0:T(1,128)}, f32[1,128]{1,0:T(1,128)}) custom-call(s32[3]{0:T(128)S(1)} %pad_add_fusion.refs_0_, bf16[1152,128]{1,0:T(8,128)(2,1)S(1)} %constant_dynamic-update-slice_fusion.refs_1_, bf16[1152,128]{1,0:T(8,128)(2,1)S(1)} %collective-permute-done.25.refs_2_, ...), custom_call_target="tpu_custom_call" | custom-call | tf_op jit(solution)/shard_map/finish/pallas_call | solution.py:483
  (90 shorter events, 21.0 us)
Async XLA Ops:
  4.6 23.7 %all-to-all-start = ((bf16[32,24,512]{2,1,0:T(8,128)(2,1)}), bf16[32,24,512]{2,1,0:T(8,128)(2,1)S(1)}, u32[]{:S(2)}, u32[]{:S(2)}) async-start(bf16[32,24,512]{2,1,0:T(8,128)(2,1)} %bitcast.5), calls=%async_computation | async-start | bytes 1572864 | tf_op jit(solution)/shard_map/all_to_all | solution.py:402
  14.0 11.3 %collective-permute-start.7 = (bf16[80,512]{1,0:T(8,128)(2,1)S(1)}, bf16[80,512]{1,0:T(8,128)(2,1)S(1)}, u32[]{:S(2)}, u32[]{:S(2)}) collective-permute-start(bf16[80,512]{1,0:T(8,128)(2,1)S(1)} %fusion.2.right_m), channel_id=1, source_target_pairs={{0,31},{1,2},{2,1},{3,4},{4,3},{5,6},{6,5},{7,8},{8,7},{9,10},{10,... | collective-permute-start | bytes 245768 | tf_op jit(solution)/shard_map/ppermute | solution.py:384
  41.3 7.1 %collective-permute-start.9 = (bf16[256,512]{1,0:T(8,128)(2,1)S(1)}, bf16[256,512]{1,0:T(8,128)(2,1)S(1)}, u32[]{:S(2)}, u32[]{:S(2)}) collective-permute-start(bf16[256,512]{1,0:T(8,128)(2,1)S(1)} %get-tuple-element.20), channel_id=1, source_target_pairs={{0,1},{1,0},{2,3},{3,2},{4,5},{5,4},{6,7},{7,6},{8,9},{9,8},{10,11... | collective-permute-start | bytes 786440 | tf_op jit(solution)/shard_map/ppermute | solution.py:384
  43.6 6.5 %collective-permute-start.5 = (bf16[64,1024]{1,0:T(8,128)(2,1)S(1)}, bf16[64,1024]{1,0:T(8,128)(2,1)S(1)}, u32[]{:S(2)}, u32[]{:S(2)}) collective-permute-start(bf16[64,1024]{1,0:T(8,128)(2,1)S(1)} %bitcast.25), channel_id=1, source_target_pairs={{0,4},{1,5},{2,6},{3,7},{4,0},{5,1},{6,2},{7,3},{8,12},{9,13},{10,... | collective-permute-start | bytes 393224 | tf_op jit(solution)/shard_map/ppermute | solution.py:384
  44.8 8.8 %collective-permute-start.3 = (bf16[64,1024]{1,0:T(8,128)(2,1)S(1)}, bf16[64,1024]{1,0:T(8,128)(2,1)S(1)}, u32[]{:S(2)}, u32[]{:S(2)}) collective-permute-start(bf16[64,1024]{1,0:T(8,128)(2,1)S(1)} %bitcast.26), channel_id=1, source_target_pairs={{0,6},{1,7},{2,0},{3,1},{4,2},{5,3},{6,4},{7,5},{8,14},{9,15},{10,... | collective-permute-start | bytes 393224 | tf_op jit(solution)/shard_map/ppermute | solution.py:384
  44.8 8.9 %collective-permute-start.1 = (bf16[64,1024]{1,0:T(8,128)(2,1)S(1)}, bf16[64,1024]{1,0:T(8,128)(2,1)S(1)}, u32[]{:S(2)}, u32[]{:S(2)}) collective-permute-start(bf16[64,1024]{1,0:T(8,128)(2,1)S(1)} %bitcast.27), channel_id=1, source_target_pairs={{0,2},{1,3},{2,4},{3,5},{4,6},{5,7},{6,0},{7,1},{8,10},{9,11},{10,... | collective-permute-start | bytes 393224 | tf_op jit(solution)/shard_map/ppermute | solution.py:384
  46.2 8.3 %collective-permute-start.11 = (bf16[64,512]{1,0:T(8,128)(2,1)S(1)}, bf16[64,512]{1,0:T(8,128)(2,1)S(1)}, u32[]{:S(2)}, u32[]{:S(2)}) collective-permute-start(bf16[64,512]{1,0:T(8,128)(2,1)S(1)} %get-tuple-element.21), channel_id=1, source_target_pairs={{1,3},{3,5},{5,7},{7,9},{9,11},{11,13},{13,15},{15,17},{17,19},{19... | collective-permute-start | bytes 196616 | tf_op jit(solution)/shard_map/ppermute | solution.py:439
  48.4 6.2 %collective-permute-start.10 = (bf16[64,512]{1,0:T(8,128)(2,1)S(1)}, bf16[64,512]{1,0:T(8,128)(2,1)S(1)}, u32[]{:S(2)}, u32[]{:S(2)}) collective-permute-start(bf16[64,512]{1,0:T(8,128)(2,1)S(1)} %get-tuple-element.21), channel_id=1, source_target_pairs={{0,31},{1,2},{2,1},{3,4},{4,3},{5,6},{6,5},{7,8},{8,7},{9,10},{10,... | collective-permute-start | bytes 196616 | tf_op jit(solution)/shard_map/ppermute | solution.py:384
  50.0 5.3 %collective-permute-start = (bf16[64,1024]{1,0:T(8,128)(2,1)S(1)}, bf16[64,1024]{1,0:T(8,128)(2,1)S(1)}, u32[]{:S(2)}, u32[]{:S(2)}) collective-permute-start(bf16[64,1024]{1,0:T(8,128)(2,1)S(1)} %bitcast.28), channel_id=1, source_target_pairs={{0,1},{1,0},{2,3},{3,2},{4,5},{5,4},{6,7},{7,6},{8,9},{9,8},{10,11... | collective-permute-start | bytes 393224 | tf_op jit(solution)/shard_map/ppermute | solution.py:384
  54.7 4.7 %collective-permute-start.14 = (bf16[256,128]{1,0:T(8,128)(2,1)S(1)}, bf16[256,128]{1,0:T(8,128)(2,1)S(1)}, u32[]{:S(2)}, u32[]{:S(2)}) collective-permute-start(bf16[256,128]{1,0:T(8,128)(2,1)S(1)} %get-tuple-element.35), channel_id=1, source_target_pairs={{0,4},{1,5},{2,6},{3,7},{4,0},{5,1},{6,2},{7,3},{8,12},{9,13},{10,... | collective-permute-start | bytes 196616 | tf_op jit(solution)/shard_map/ppermute | solution.py:384
  57.0 5.0 %collective-permute-start.12 = (bf16[256,128]{1,0:T(8,128)(2,1)S(1)}, bf16[256,128]{1,0:T(8,128)(2,1)S(1)}, u32[]{:S(2)}, u32[]{:S(2)}) collective-permute-start(bf16[256,128]{1,0:T(8,128)(2,1)S(1)} %get-tuple-element.37), channel_id=1, source_target_pairs={{0,2},{1,3},{2,4},{3,5},{4,6},{5,7},{6,0},{7,1},{8,10},{9,11},{10,... | collective-permute-start | bytes 196616 | tf_op jit(solution)/shard_map/ppermute | solution.py:384
  62.6 5.6 %collective-permute-start.15 = (bf16[288,128]{1,0:T(8,128)(2,1)S(1)}, bf16[288,128]{1,0:T(8,128)(2,1)S(1)}, u32[]{:S(2)}, u32[]{:S(2)}) collective-permute-start(bf16[288,128]{1,0:T(8,128)(2,1)S(1)} %get-tuple-element.32), channel_id=1, source_target_pairs={{0,8},{1,9},{2,10},{3,11},{4,12},{5,13},{6,14},{7,15},{8,16},{9,17... | collective-permute-start | bytes 221192 | tf_op jit(solution)/shard_map/ppermute | solution.py:384
  63.6 7.2 %collective-permute-start.17 = (bf16[288,128]{1,0:T(8,128)(2,1)S(1)}, bf16[288,128]{1,0:T(8,128)(2,1)S(1)}, u32[]{:S(2)}, u32[]{:S(2)}) collective-permute-start(bf16[288,128]{1,0:T(8,128)(2,1)S(1)} %get-tuple-element.33), channel_id=1, source_target_pairs={{0,16},{1,17},{2,18},{3,19},{4,20},{5,21},{6,22},{7,23},{8,24},{9,... | collective-permute-start | bytes 221192 | tf_op jit(solution)/shard_map/ppermute | solution.py:384
  74.4 12.2 %collective-permute-start.21 = (bf16[288,128]{1,0:T(8,128)(2,1)S(1)}, bf16[288,128]{1,0:T(8,128)(2,1)S(1)}, u32[]{:S(2)}, u32[]{:S(2)}) collective-permute-start(bf16[288,128]{1,0:T(8,128)(2,1)S(1)} %add_convert_fusion.2), channel_id=1, source_target_pairs={{0,128},{32,160},{64,192},{96,224},{128,0},{160,32},{192,64},{224,... | collective-permute-start | bytes 221192 | tf_op jit(solution)/shard_map/ppermute | solution.py:399
  81.9 5.7 %collective-permute-start.20 = (bf16[288,128]{1,0:T(8,128)(2,1)S(1)}, bf16[288,128]{1,0:T(8,128)(2,1)S(1)}, u32[]{:S(2)}, u32[]{:S(2)}) collective-permute-start(bf16[288,128]{1,0:T(8,128)(2,1)S(1)} %add_convert_fusion.2), channel_id=1, source_target_pairs={{0,192},{32,224},{64,0},{96,32},{128,64},{160,96},{192,128},{224,1... | collective-permute-start | bytes 221192 | tf_op jit(solution)/shard_map/ppermute | solution.py:399
  81.9 5.8 %collective-permute-start.19 = (bf16[288,128]{1,0:T(8,128)(2,1)S(1)}, bf16[288,128]{1,0:T(8,128)(2,1)S(1)}, u32[]{:S(2)}, u32[]{:S(2)}) collective-permute-start(bf16[288,128]{1,0:T(8,128)(2,1)S(1)} %add_convert_fusion.2), channel_id=1, source_target_pairs={{0,64},{32,96},{64,128},{96,160},{128,192},{160,224},{192,0},{224,... | collective-permute-start | bytes 221192 | tf_op jit(solution)/shard_map/ppermute | solution.py:399
  87.7 7.0 %collective-permute-start.24 = (bf16[288,128]{1,0:T(8,128)(2,1)S(1)}, bf16[288,128]{1,0:T(8,128)(2,1)S(1)}, u32[]{:S(2)}, u32[]{:S(2)}) collective-permute-start(bf16[288,128]{1,0:T(8,128)(2,1)S(1)} %add_convert_fusion.1), channel_id=1, source_target_pairs={{0,16},{1,17},{2,18},{3,19},{4,20},{5,21},{6,22},{7,23},{8,24},{9,... | collective-permute-start | bytes 221192 | tf_op jit(solution)/shard_map/ppermute | solution.py:384
  89.3 5.4 %collective-permute-start.23 = (bf16[288,128]{1,0:T(8,128)(2,1)S(1)}, bf16[288,128]{1,0:T(8,128)(2,1)S(1)}, u32[]{:S(2)}, u32[]{:S(2)}) collective-permute-start(bf16[288,128]{1,0:T(8,128)(2,1)S(1)} %add_convert_fusion.1), channel_id=1, source_target_pairs={{0,24},{1,25},{2,26},{3,27},{4,28},{5,29},{6,30},{7,31},{8,0},{9,1... | collective-permute-start | bytes 221192 | tf_op jit(solution)/shard_map/ppermute | solution.py:384
  90.2 4.4 %collective-permute-start.22 = (bf16[288,128]{1,0:T(8,128)(2,1)S(1)}, bf16[288,128]{1,0:T(8,128)(2,1)S(1)}, u32[]{:S(2)}, u32[]{:S(2)}) collective-permute-start(bf16[288,128]{1,0:T(8,128)(2,1)S(1)} %add_convert_fusion.1), channel_id=1, source_target_pairs={{0,8},{1,9},{2,10},{3,11},{4,12},{5,13},{6,14},{7,15},{8,16},{9,17... | collective-permute-start | bytes 221192 | tf_op jit(solution)/shard_map/ppermute | solution.py:384
  94.7 9.3 %collective-permute-start.27 = (bf16[1152,128]{1,0:T(8,128)(2,1)S(1)}, bf16[1152,128]{1,0:T(8,128)(2,1)S(1)}, u32[]{:S(2)}, u32[]{:S(2)}) collective-permute-start(bf16[1152,128]{1,0:T(8,128)(2,1)S(1)} %constant_dynamic-update-slice_fusion.refs_1_), channel_id=1, source_target_pairs={{0,4},{1,5},{2,6},{3,7},{4,0},{5,1},{6,2},{7,3},{8,12},{9,13},{10,... | collective-permute-start | bytes 884744 | tf_op jit(solution)/shard_map/ppermute | solution.py:384
  95.4 13.6 %collective-permute-start.26 = (bf16[1152,128]{1,0:T(8,128)(2,1)S(1)}, bf16[1152,128]{1,0:T(8,128)(2,1)S(1)}, u32[]{:S(2)}, u32[]{:S(2)}) collective-permute-start(bf16[1152,128]{1,0:T(8,128)(2,1)S(1)} %constant_dynamic-update-slice_fusion.refs_1_), channel_id=1, source_target_pairs={{0,6},{1,7},{2,0},{3,1},{4,2},{5,3},{6,4},{7,5},{8,14},{9,15},{10,... | collective-permute-start | bytes 884744 | tf_op jit(solution)/shard_map/ppermute | solution.py:384
  96.8 13.8 %collective-permute-start.25 = (bf16[1152,128]{1,0:T(8,128)(2,1)S(1)}, bf16[1152,128]{1,0:T(8,128)(2,1)S(1)}, u32[]{:S(2)}, u32[]{:S(2)}) collective-permute-start(bf16[1152,128]{1,0:T(8,128)(2,1)S(1)} %constant_dynamic-update-slice_fusion.refs_1_), channel_id=1, source_target_pairs={{0,2},{1,3},{2,4},{3,5},{4,6},{5,7},{6,0},{7,1},{8,10},{9,11},{10,... | collective-permute-start | bytes 884744 | tf_op jit(solution)/shard_map/ppermute | solution.py:384
  96.9 15.2 %collective-permute-start.28 = (bf16[1152,128]{1,0:T(8,128)(2,1)S(1)}, bf16[1152,128]{1,0:T(8,128)(2,1)S(1)}, u32[]{:S(2)}, u32[]{:S(2)}) collective-permute-start(bf16[1152,128]{1,0:T(8,128)(2,1)S(1)} %constant_dynamic-update-slice_fusion.refs_1_), channel_id=1, source_target_pairs={{0,1},{1,0},{2,3},{3,2},{4,5},{5,4},{6,7},{7,6},{8,9},{9,8},{10,11... | collective-permute-start | bytes 884744 | tf_op jit(solution)/shard_map/ppermute | solution.py:384
  104.0 8.1 %collective-permute-start.31 = (bf16[1152,128]{1,0:T(8,128)(2,1)S(1)}, bf16[1152,128]{1,0:T(8,128)(2,1)S(1)}, u32[]{:S(2)}, u32[]{:S(2)}) collective-permute-start(bf16[1152,128]{1,0:T(8,128)(2,1)S(1)} %collective-permute-done.27.refs_4_), channel_id=1, source_target_pairs={{0,1},{1,0},{2,3},{3,2},{4,5},{5,4},{6,7},{7,6},{8,9},{9,8},{10,11... | collective-permute-start | bytes 884744 | tf_op jit(solution)/shard_map/ppermute | solution.py:384
  (19 other events, 145.6 us)
